TPU v7x, 32 devices: a whole 2x2x4 slice. The times are simulated.
32 devices in a mesh: dp: 8 (over z, y), fsdp: 4 (over x, core).
Axes of the slice: x: 2, y: 2, z: 4, core: 2. Of those that a mesh axis runs over, the one named last changes fastest.
Arguments:
- tokens: bfloat16 [4096, 896], P(('dp', 'fsdp')), may hold values from -6 to 6
- cotangent: bfloat16 [4096, 896], P(('dp', 'fsdp')), may hold values from -6 to 6
- segments: int32 [32, 128], P(('dp', 'fsdp')), may hold values from 0 to 7, never falling along the last dimension, each value on 1 to 64 neighbouring positions
- gain_att: float32 [896], replicated, may hold values from 0.5 to 1.5
- gain_ffn: float32 [896], replicated, may hold values from 0.5 to 1.5
- qkv_bias: float32 [1152], replicated, may hold values from -3 to 3
- w_attention: bfloat16 [2048, 896], P(('dp', 'fsdp')), may hold values from -0.31 to 0.31
- w_gate: bfloat16 [4864, 896], P(('dp', 'fsdp')), may hold values from -0.1875 to 0.1875
- w_up: bfloat16 [4864, 896], P(('dp', 'fsdp')), may hold values from -0.1875 to 0.1875
- w_down: bfloat16 [4864, 896], P(('dp', 'fsdp')), may hold values from -0.078125 to 0.078125
Outputs:
- layer_out: bfloat16 [4096, 896], P(('dp', 'fsdp'))
- grad_tokens: bfloat16 [4096, 896], P(('dp', 'fsdp'))
- grad_gainatt: float32 [896], replicated
- grad_gainffn: float32 [896], replicated
- grad_bias: float32 [1152], replicated
- grad_attention: float32 [2048, 896], P(('dp', 'fsdp'))
- grad_gate: float32 [4864, 896], P(('dp', 'fsdp'))
- grad_up: float32 [4864, 896], P(('dp', 'fsdp'))
- grad_down: float32 [4864, 896], P(('dp', 'fsdp'))
Inputs may be any that keep to these rules, and one draw needn't show every extreme that they name: `segments`: in each device's row of 128 tokens the numbers never fall; each device holds exactly 8 sequences, each of 1 to 64 tokens.
All inputs are finite; a program needn't handle non-finite values.
Results may differ from a plain program's by a relative error of at most 0.012.
The roundings to bfloat16 on the way count: a program that leaves them out, or rounds other values in their place, can miss the bound.
Values may be sent and summed in bfloat16 or wider, within the bound.
A program may use at most 320 MiB of HBM per device.

v0:
```python
import jax
import jax.numpy as jnp
from jax import lax
from jax.sharding import PartitionSpec as P

HEADS = 14
KV_HEADS = 2
HEAD_DIM = 64
QKV = 1152


EPS = 1e-06
THETA = 1000000.0


def rotary_tables(segments):
    length = segments.shape[-1]
    before = jnp.sum((segments[..., None, :] < segments[..., :, None]).astype(jnp.int32), -1)
    positions = jnp.arange(length, dtype=jnp.int32)[None, :] - before
    halfway = HEAD_DIM // 2
    frequency = THETA ** (-2.0 * jnp.arange(halfway, dtype=jnp.float32) / HEAD_DIM)
    angles = positions.astype(jnp.float32)[..., None] * frequency
    cosine = jnp.concatenate([jnp.cos(angles), jnp.cos(angles)], -1)[:, :, None, :]
    sines = jnp.concatenate([jnp.sin(angles), jnp.sin(angles)], -1)[:, :, None, :]
    return (cosine, sines)


def rotate(tensor):
    halfway = tensor.shape[-1] // 2
    return jnp.concatenate([-tensor[..., halfway:], tensor[..., :halfway]], -1)


def unrotate(tensor):
    halfway = tensor.shape[-1] // 2
    return jnp.concatenate([tensor[..., halfway:], -tensor[..., :halfway]], -1)


def visible(segments):
    length = segments.shape[-1]
    matches = segments[..., :, None] == segments[..., None, :]
    index = jnp.arange(length, dtype=jnp.int32)
    causal = index[None, :] <= index[:, None]
    return matches & causal[None]


def attend_scores(query_bf, key_bf, allowed):
    scores = jnp.einsum(
        "grkpd,gskd->gkprs", query_bf, key_bf, preferred_element_type=jnp.float32
    ) * HEAD_DIM ** (-0.5)
    return jnp.where(allowed[:, None, None], scores, -1e30)


def norm_back(grad_in, values, scale, gain):
    weighted = grad_in * gain
    return scale * weighted - values * scale**3 * jnp.mean(weighted * values, -1, keepdims=True)


def plain_dot(left, right):
    return jnp.dot(left, right, preferred_element_type=jnp.float32)


def proj_dot(left, right):
    return lax.dot_general(
        left, right, (((1,), (1,)), ((), ())), preferred_element_type=jnp.float32
    )


def outer_dot(left, right):
    return lax.dot_general(
        left, right, (((0,), (0,)), ((), ())), preferred_element_type=jnp.float32
    )


def collect(w_attention, w_gate, w_up, w_down):
    return (
        lax.all_gather(w_attention, ("dp", "fsdp"), axis=0, tiled=True),
        lax.all_gather(w_gate, ("dp", "fsdp"), axis=0, tiled=True),
        lax.all_gather(w_up, ("dp", "fsdp"), axis=0, tiled=True),
        lax.all_gather(w_down, ("dp", "fsdp"), axis=0, tiled=True),
    )


def on_device(
    tokens, cotangent, segments, gain_att, gain_ffn, qkv_bias, w_attention, w_gate, w_up, w_down
):
    gathered = collect(w_attention, w_gate, w_up, w_down)
    rows_here = tokens.shape[0]
    q_width = HEADS * HEAD_DIM
    kv_width = KV_HEADS * HEAD_DIM
    repeat_count = HEADS // KV_HEADS
    resid_in = tokens.astype(jnp.float32)
    scale_att = lax.rsqrt(jnp.mean(resid_in * resid_in, -1, keepdims=True) + EPS)
    normed_att = (resid_in * scale_att * gain_att).astype(jnp.bfloat16)
    projected = proj_dot(normed_att, gathered[0][:QKV]) + qkv_bias
    cosine, sines = rotary_tables(segments)
    queries = projected[:, :q_width].reshape(1, rows_here, HEADS, HEAD_DIM)
    keys_raw = projected[:, q_width : q_width + kv_width].reshape(1, rows_here, KV_HEADS, HEAD_DIM)
    values_raw = projected[:, q_width + kv_width :].reshape(1, rows_here, KV_HEADS, HEAD_DIM)
    query_bf = (
        (queries * cosine + rotate(queries) * sines)
        .astype(jnp.bfloat16)
        .reshape(1, rows_here, KV_HEADS, repeat_count, HEAD_DIM)
    )
    key_bf = (keys_raw * cosine + rotate(keys_raw) * sines).astype(jnp.bfloat16)
    value_bf = values_raw.astype(jnp.bfloat16)
    allowed = visible(segments)
    scores = attend_scores(query_bf, key_bf, allowed)
    log_total = jnp.log(jnp.sum(jnp.exp(scores), -1, keepdims=True))
    soft_bf = jnp.exp(scores - log_total).astype(jnp.bfloat16)
    attended = jnp.einsum(
        "gkprs,gskd->grkpd", soft_bf, value_bf, preferred_element_type=jnp.float32
    )
    attended = attended.reshape(rows_here, q_width).astype(jnp.bfloat16)
    middle = resid_in + plain_dot(attended, gathered[0][QKV:])
    scale_ffn = lax.rsqrt(jnp.mean(middle * middle, -1, keepdims=True) + EPS)
    normed_ffn = (middle * scale_ffn * gain_ffn).astype(jnp.bfloat16)
    gate_pre = proj_dot(normed_ffn, gathered[1])
    up_pre = proj_dot(normed_ffn, gathered[2])
    sigmoid_gate = jax.nn.sigmoid(gate_pre)
    hidden_act = (gate_pre * sigmoid_gate * up_pre).astype(jnp.bfloat16)
    down_part = plain_dot(hidden_act, gathered[3])
    weights_back = collect(w_attention, w_gate, w_up, w_down)
    grad_hidden = proj_dot(cotangent, weights_back[3])
    gate_back = (
        grad_hidden * up_pre * sigmoid_gate * (1.0 + gate_pre * (1.0 - sigmoid_gate))
    ).astype(jnp.bfloat16)
    up_back = (grad_hidden * gate_pre * sigmoid_gate).astype(jnp.bfloat16)
    normed_part = plain_dot(gate_back, weights_back[1]) + plain_dot(up_back, weights_back[2])
    layer_out = (middle + down_part).astype(jnp.bfloat16)
    grad_middle = cotangent.astype(jnp.float32) + norm_back(
        normed_part, middle, scale_ffn, gain_ffn
    )
    middle_bf = grad_middle.astype(jnp.bfloat16)
    grad_attended = proj_dot(middle_bf, weights_back[0][QKV:]).astype(jnp.bfloat16)
    grad_attended = grad_attended.reshape(1, rows_here, KV_HEADS, repeat_count, HEAD_DIM)
    scores_again = attend_scores(query_bf, key_bf, allowed)
    soft = jnp.exp(scores_again - log_total)
    grad_soft = jnp.einsum(
        "grkpd,gskd->gkprs", grad_attended, value_bf, preferred_element_type=jnp.float32
    )
    grad_scores = (
        soft * (grad_soft - jnp.sum(soft * grad_soft, -1, keepdims=True)) * HEAD_DIM ** (-0.5)
    ).astype(jnp.bfloat16)
    grad_queries = jnp.einsum(
        "gkprs,gskd->grkpd", grad_scores, key_bf, preferred_element_type=jnp.float32
    )
    grad_queries = grad_queries.reshape(1, rows_here, HEADS, HEAD_DIM)
    grad_keys = jnp.einsum(
        "gkprs,grkpd->gskd", grad_scores, query_bf, preferred_element_type=jnp.float32
    )
    grad_values = jnp.einsum(
        "gkprs,grkpd->gskd",
        soft.astype(jnp.bfloat16),
        grad_attended,
        preferred_element_type=jnp.float32,
    )
    grad_queries = grad_queries * cosine + unrotate(grad_queries * sines)
    grad_keys = grad_keys * cosine + unrotate(grad_keys * sines)
    grad_projected = jnp.concatenate(
        [
            grad_queries.reshape(rows_here, q_width),
            grad_keys.reshape(rows_here, kv_width),
            grad_values.reshape(rows_here, kv_width),
        ],
        -1,
    )
    projected_bf = grad_projected.astype(jnp.bfloat16)
    grad_inputs = plain_dot(projected_bf, weights_back[0][:QKV])
    grad_tokens = (grad_middle + norm_back(grad_inputs, resid_in, scale_att, gain_att)).astype(
        jnp.bfloat16
    )
    attention_term = jnp.concatenate(
        [outer_dot(projected_bf, normed_att), outer_dot(attended, middle_bf)], 0
    )
    grad_attention = lax.psum_scatter(
        attention_term, ("dp", "fsdp"), scatter_dimension=0, tiled=True
    )
    feed_grads = lax.psum_scatter(
        jnp.stack(
            [
                outer_dot(gate_back, normed_ffn),
                outer_dot(up_back, normed_ffn),
                outer_dot(hidden_act, cotangent),
            ],
            1,
        ),
        ("dp", "fsdp"),
        scatter_dimension=0,
        tiled=True,
    )
    small_sums = lax.psum(
        (
            jnp.sum(grad_inputs * resid_in * scale_att, 0),
            jnp.sum(normed_part * middle * scale_ffn, 0),
            jnp.sum(grad_projected, 0),
        ),
        ("dp", "fsdp"),
    )
    return (
        layer_out,
        grad_tokens,
        small_sums[0],
        small_sums[1],
        small_sums[2],
        grad_attention,
        feed_grads[:, 0],
        feed_grads[:, 1],
        feed_grads[:, 2],
    )


def solution(mesh):
    placed = (
        P(("dp", "fsdp"), None),
        P(("dp", "fsdp"), None),
        P(("dp", "fsdp"), None),
        P(),
        P(),
        P(),
        P(("dp", "fsdp"), None),
        P(("dp", "fsdp"), None),
        P(("dp", "fsdp"), None),
        P(("dp", "fsdp"), None),
    )
    return jax.shard_map(
        on_device,
        mesh=mesh,
        in_specs=placed,
        out_specs=(
            P(("dp", "fsdp"), None),
            P(("dp", "fsdp"), None),
            P(),
            P(),
            P(),
            P(("dp", "fsdp"), None),
            P(("dp", "fsdp"), None),
            P(("dp", "fsdp"), None),
            P(("dp", "fsdp"), None),
        ),
        check_vma=False,
    )
```

profile of v0, /device:TPU:0, one launch (start us, length us, event | category | flops | bytes accessed | tf_op | source)
XLA Modules:
  0.0 1094.6 jit_solution(12169329613476941089)
XLA Ops:
  7.2 0.0 all-gather.5.cloned.1.call-start
  7.2 0.7 all-gather.5.cloned.1.call-update
  7.9 0.0 all-gather.9.cloned.1.call-start
  8.0 0.7 all-gather.9.cloned.1.call-update
  8.7 0.0 all-gather.7.cloned.1.call-start
  8.7 0.7 all-gather.7.cloned.1.call-update
  9.4 0.0 all-gather.11.cloned.1.call-start
  9.4 0.5 all-gather.11.cloned.1.call-update
  10.0 0.0 reduce-scatter.5.cloned.1.call-start
  10.0 0.9 convert_reduce_fusion
  10.9 0.1 multiply_cosine_fusion
  11.1 1.1 fusion.19
  12.2 0.5 multiply_multiply_fusion
  12.8 0.8 fusion.42
  13.6 60.4 %all-gather.5.cloned.1.call-done = bf16[2048,896]{1,0:T(8,128)(2,1)} async-done(((bf16[64,896]{1,0:T(8,128)(2,1)}), bf16[2048,896]{1,0:T(8,128)(2,1)}) %all-gather.5.cloned.1.call-update) | async-done | bytes 3670032 | tf_op jit(solution)/shard_map/all_gather | solution.py:76
  74.0 2.5 convolution_add_fusion
  76.6 0.1 copy.43
  76.7 0.2 copy.46
  76.9 0.1 copy.44
  77.1 0.1 fusion.30
  77.2 0.4 exponential_reduce_fusion
  77.7 0.3 convolution_convert_fusion
  77.9 0.0 copy-done.4
  78.0 2.0 multiply_reduce_fusion.3
  80.0 0.1 multiply_convert_fusion.4
  80.2 73.7 %all-gather.9.cloned.1.call-done = bf16[4864,896]{1,0:T(8,128)(2,1)} async-done(((bf16[152,896]{1,0:T(8,128)(2,1)}), bf16[4864,896]{1,0:T(8,128)(2,1)}) %all-gather.9.cloned.1.call-update) | async-done | bytes 8716304 | tf_op jit(solution)/shard_map/all_gather | solution.py:78
  153.8 7.4 fusion.53
  161.2 72.5 %all-gather.7.cloned.1.call-done = bf16[4864,896]{1,0:T(8,128)(2,1)} async-done(((bf16[152,896]{1,0:T(8,128)(2,1)}), bf16[4864,896]{1,0:T(8,128)(2,1)}) %all-gather.7.cloned.1.call-update) | async-done | bytes 8716304 | tf_op jit(solution)/shard_map/all_gather | solution.py:77
  233.8 7.4 fusion.52
  241.2 72.4 %all-gather.11.cloned.1.call-done = bf16[4864,896]{1,0:T(8,128)(2,1)} async-done(((bf16[152,896]{1,0:T(8,128)(2,1)}), bf16[4864,896]{1,0:T(8,128)(2,1)}) %all-gather.11.cloned.1.call-update) | async-done | bytes 8716304 | tf_op jit(solution)/shard_map/all_gather | solution.py:79
  313.6 7.5 multiply_convert_fusion
  321.1 7.3 convolution_bitcast_fusion
  328.4 7.4 convolution_bitcast_fusion.1
  335.8 7.3 convolution_bitcast_fusion.2
  343.0 34.6 %pad_maximum_fusion = f32[4864,3,896]{2,0,1:T(8,128)} fusion(f32[4864,1,896]{2,0,1:T(8,128)} %convolution_bitcast_fusion, f32[4864,1,896]{2,0,1:T(8,128)} %convolution_bitcast_fusion.1, f32[4864,1,896]{2,0,1:T(8,128)} %convolution_bitcast_fusion.2), kind=kLoop, calls=%fused_computation | loop fusion | flops 26148864 | bytes 104595456 | tf_op jit(solution)/shard_map/stack | solution.py:179
  377.6 0.0 reduce-scatter.5.cloned.1.call-update
  377.7 0.2 reduce-scatter.3.cloned.1.call-start
  377.9 5.0 fusion.54
  383.0 5.4 multiply_reduce_fusion.1
  388.3 0.2 subtract_add_fusion
  388.5 2.0 fusion.13
  390.5 0.2 copy.49
  390.7 0.3 multiply_reduce_fusion
  391.1 0.2 fusion.18
  391.3 0.2 fusion.55
  391.7 0.1 copy-done.13
  391.8 0.1 fusion.31
  391.9 0.4 copy-done.11
  392.3 0.1 copy-done.15
  392.4 0.3 broadcast_multiply_fusion
  392.8 0.3 fusion.34
  393.1 0.6 fusion.37
  393.7 0.0 copy-done.5
  393.7 0.8 fusion.43
  394.5 3.4 pad_maximum_fusion.1
  398.0 0.2 fusion.32
  398.2 0.7 copy-done.6
  398.9 2.4 fusion.28
  401.3 49.4 %all-reduce = (f32[896]{0:T(1024)}, f32[896]{0:T(1024)}, f32[1152]{0:T(1024)}) all-reduce(f32[896]{0:T(1024)S(1)} %get-tuple-element.11, f32[896]{0:T(1024)S(1)} %get-tuple-element.9, f32[1152]{0:T(1024)S(1)} %fusion.32), channel_id=1, replica_groups=mesh['dp'=8,'fsdp'=4] {'dp','fsdp'}, use_global_device_ids=true, to_apply=%region_8.9 | all-reduce | flops 2944 | bytes 23552 | tf_op jit(solution)/shard_map/psum | solution.py:191
  450.7 0.9 fusion.25
  451.6 5.8 fusion.12
  457.4 470.0 %reduce-scatter.5.cloned.1.call-done = f32[152,3,896]{2,0,1:T(8,128)} async-done(((f32[4864,3,896]{2,0,1:T(8,128)}), f32[152,3,896]{2,0,1:T(8,128)}) %reduce-scatter.5.cloned.1.call-update) | async-done | bytes 1634320 | tf_op jit(solution)/shard_map/reduce_scatter | solution.py:178
  927.4 2.6 slice_bitcast_fusion
  930.0 157.8 %reduce-scatter.3.cloned.1.call-done = f32[64,896]{1,0:T(8,128)} async-done(((f32[2048,896]{1,0:T(8,128)}), f32[64,896]{1,0:T(8,128)}) %reduce-scatter.3.cloned.1.call-update) | async-done | bytes 229392 | tf_op jit(solution)/shard_map/reduce_scatter | solution.py:175
  (62 shorter events, 0.4 us)
Async XLA Ops:
  7.2 66.8 %all-gather.5.cloned.1.call-start = ((), (), s32[]{:S(2)}) async-start(), calls=%async_computation.2 | async-start | bytes 3784704 | tf_op jit(solution)/shard_map/all_gather | solution.py:76
  7.9 145.9 %all-gather.9.cloned.1.call-start = ((), (), s32[]{:S(2)}) async-start(), calls=%async_computation.4 | async-start | bytes 8988672 | tf_op jit(solution)/shard_map/all_gather | solution.py:78
  8.7 225.1 %all-gather.7.cloned.1.call-start = ((), (), s32[]{:S(2)}) async-start(), calls=%async_computation.3 | async-start | bytes 8988672 | tf_op jit(solution)/shard_map/all_gather | solution.py:77
  9.4 304.2 %all-gather.11.cloned.1.call-start = ((), (), s32[]{:S(2)}) async-start(), calls=%async_computation.5 | async-start | bytes 8988672 | tf_op jit(solution)/shard_map/all_gather | solution.py:79
  10.0 917.5 %reduce-scatter.5.cloned.1.call-start = ((), (), s32[]{:S(2)}) async-start(), calls=%async_computation.7 | async-start | bytes 53932032 | tf_op jit(solution)/shard_map/reduce_scatter | solution.py:178
  11.1 66.0 %copy-start.12 = (f32[128,64]{0,1:T(8,128)}, f32[128,64]{0,1:T(8,128)S(1)}, u32[]{:S(2)}) copy-start(f32[128,64]{0,1:T(8,128)S(1)} %maximum_bitcast_fusion) | copy-start | bytes 98308
  11.1 380.4 %copy-start.14 = (f32[128,64]{0,1:T(8,128)}, f32[128,64]{0,1:T(8,128)S(1)}, u32[]{:S(2)}) copy-start(f32[128,64]{0,1:T(8,128)S(1)} %maximum_bitcast_fusion.1) | copy-start | bytes 98308
  12.7 63.8 %copy-start.20 = (f32[128]{0:T(128)}, f32[128]{0:T(128)S(1)}, u32[]{:S(2)}) copy-start(f32[128]{0:T(128)S(1)} %get-tuple-element.33) | copy-start | bytes 1540
  77.0 0.9 copy-start.4
  77.2 2.8 copy-start.10
  77.2 2.8 copy-start.18
  77.9 2.1 copy-start.7
  161.2 152.3 %copy-start.9 = (bf16[128,896]{1,0:T(8,128)(2,1)S(1)}, bf16[128,896]{1,0:T(8,128)(2,1)}, u32[]{:S(2)}) copy-start(bf16[128,896]{1,0:T(8,128)(2,1)} %param.11) | copy-start | bytes 688132
  321.1 7.3 copy-start
  321.1 7.3 copy-start.2
  377.7 710.1 %reduce-scatter.3.cloned.1.call-start = ((), (), s32[]{:S(2)}) async-start(), calls=%async_computation.6 | async-start | bytes 7569408 | tf_op jit(solution)/shard_map/reduce_scatter | solution.py:175
  377.9 5.1 copy-start.3
  391.1 0.8 copy-start.13
  391.3 1.0 copy-start.11
  391.6 0.8 copy-start.15
  391.6 1.4 copy-start.8
  392.7 5.2 copy-start.16
  392.7 1.0 copy-start.5
  392.8 1.0 copy-start.19
  392.8 0.9 copy-start.21
  393.1 4.9 copy-start.17
  397.9 1.0 copy-start.6
  397.9 1.0 copy-start.22
  398.0 52.8 %copy-start.23 = (f32[128]{0:T(128)S(1)}, f32[128]{0:T(128)}, u32[]{:S(2)}) copy-start(f32[128]{0:T(128)} %get-tuple-element.32) | copy-start | bytes 1540
  398.9 52.8 %copy-start.1 = (bf16[128,4864]{1,0:T(8,128)(2,1)S(1)}, bf16[128,4864]{1,0:T(8,128)(2,1)}, u32[]{:S(2)}) copy-start(bf16[128,4864]{1,0:T(8,128)(2,1)} %copy-done) | copy-start | bytes 3735556
Sparse Core Ops, SparseCore 0:
  10.8 63.1 all-gather.4
  76.9 76.8 all-gather.8
  156.8 76.9 all-gather.6
  236.6 76.9 all-gather.10
  377.8 549.6 reduce-scatter.4
  930.2 157.5 reduce-scatter.2
where the time goes:
time: 1100 us; the launch traced here: 1090 us
  waiting for transfers between devices  909 us (83%)
  matrix products  72.5 us (7%)
  blocking collectives  49.4 us (4%)
  other arithmetic  43.5 us (4%)
  between operations  14.6 us (1%)
    reduce_scatter x1, waiting for transfers between devices, on_device(): lax.psum_scatter(jnp.stack([outer_dot(gate_back, normed_ffn), outer_dot(u...  470 us
    reduce_scatter x1, waiting for transfers between devices, on_device(): lax.psum_scatter(attention_term, ('dp', 'fsdp'), scatter_dimension=0, til...  158 us
    all_gather x1, waiting for transfers between devices, collect(): lax.all_gather(w_up, ('dp', 'fsdp'), axis=0, tiled=True)  73.7 us
    all_gather x1, waiting for transfers between devices, collect(): lax.all_gather(w_gate, ('dp', 'fsdp'), axis=0, tiled=True)  72.5 us
    all_gather x1, waiting for transfers between devices, collect(): lax.all_gather(w_down, ('dp', 'fsdp'), axis=0, tiled=True)  72.4 us
    all_gather x1, waiting for transfers between devices, collect(): lax.all_gather(w_attention, ('dp', 'fsdp'), axis=0, tiled=True)  60.4 us
    psum x1, blocking collectives, on_device(): lax.psum((jnp.sum(grad_inputs * resid_in * scale_att, 0), jnp.sum(normed_...  49.4 us
    another operation x1, other arithmetic, on_device(): jnp.stack([outer_dot(gate_back, normed_ffn), outer_dot(up_back, normed_ff...  34.6 us
  transfers between devices with their start and end apart: 6, of which 6 were waited for; matrix products, arithmetic and copies ran while one was open for 5% of the time, Pallas kernels for 0%

commit v1 on v0

--- a/solution.py
+++ b/solution.py
@@ -71,19 +71,26 @@
     )
 
 
-def collect(w_attention, w_gate, w_up, w_down):
-    return (
-        lax.all_gather(w_attention, ("dp", "fsdp"), axis=0, tiled=True),
-        lax.all_gather(w_gate, ("dp", "fsdp"), axis=0, tiled=True),
-        lax.all_gather(w_up, ("dp", "fsdp"), axis=0, tiled=True),
-        lax.all_gather(w_down, ("dp", "fsdp"), axis=0, tiled=True),
-    )
+BOTH = ("dp", "fsdp")
+
+
+def gather(shard, axes):
+    return lax.all_gather(shard, axes, axis=0, tiled=True)
+
+
+def scatter_sum(terms, axes):
+    return lax.psum_scatter(terms, axes, scatter_dimension=0, tiled=True)
 
 
 def on_device(
     tokens, cotangent, segments, gain_att, gain_ffn, qkv_bias, w_attention, w_gate, w_up, w_down
 ):
-    gathered = collect(w_attention, w_gate, w_up, w_down)
+    w_all = gather(w_attention, BOTH)
+    w_qkv, w_out = w_all[:QKV], w_all[QKV:]
+    width = tokens.shape[1]
+    w_feed = gather(jnp.concatenate([w_gate, w_up, w_down], 1), "fsdp")
+    g_gate, g_up, g_down = w_feed[:, :width], w_feed[:, width : 2 * width], w_feed[:, 2 * width :]
+    cot_group = gather(cotangent, "dp")
     rows_here = tokens.shape[0]
     q_width = HEADS * HEAD_DIM
     kv_width = KV_HEADS * HEAD_DIM
@@ -91,7 +98,7 @@
     resid_in = tokens.astype(jnp.float32)
     scale_att = lax.rsqrt(jnp.mean(resid_in * resid_in, -1, keepdims=True) + EPS)
     normed_att = (resid_in * scale_att * gain_att).astype(jnp.bfloat16)
-    projected = proj_dot(normed_att, gathered[0][:QKV]) + qkv_bias
+    projected = proj_dot(normed_att, w_qkv) + qkv_bias
     cosine, sines = rotary_tables(segments)
     queries = projected[:, :q_width].reshape(1, rows_here, HEADS, HEAD_DIM)
     keys_raw = projected[:, q_width : q_width + kv_width].reshape(1, rows_here, KV_HEADS, HEAD_DIM)
@@ -111,27 +118,38 @@
         "gkprs,gskd->grkpd", soft_bf, value_bf, preferred_element_type=jnp.float32
     )
     attended = attended.reshape(rows_here, q_width).astype(jnp.bfloat16)
-    middle = resid_in + plain_dot(attended, gathered[0][QKV:])
+    middle = resid_in + plain_dot(attended, w_out)
     scale_ffn = lax.rsqrt(jnp.mean(middle * middle, -1, keepdims=True) + EPS)
     normed_ffn = (middle * scale_ffn * gain_ffn).astype(jnp.bfloat16)
-    gate_pre = proj_dot(normed_ffn, gathered[1])
-    up_pre = proj_dot(normed_ffn, gathered[2])
+    normed_group = gather(normed_ffn, "dp")
+    gate_pre = proj_dot(normed_group, g_gate)
+    up_pre = proj_dot(normed_group, g_up)
+    grad_hidden = proj_dot(cot_group, g_down)
     sigmoid_gate = jax.nn.sigmoid(gate_pre)
     hidden_act = (gate_pre * sigmoid_gate * up_pre).astype(jnp.bfloat16)
-    down_part = plain_dot(hidden_act, gathered[3])
-    weights_back = collect(w_attention, w_gate, w_up, w_down)
-    grad_hidden = proj_dot(cotangent, weights_back[3])
     gate_back = (
         grad_hidden * up_pre * sigmoid_gate * (1.0 + gate_pre * (1.0 - sigmoid_gate))
     ).astype(jnp.bfloat16)
     up_back = (grad_hidden * gate_pre * sigmoid_gate).astype(jnp.bfloat16)
-    normed_part = plain_dot(gate_back, weights_back[1]) + plain_dot(up_back, weights_back[2])
+    normed_terms = plain_dot(gate_back, g_gate) + plain_dot(up_back, g_up)
+    normed_part = scatter_sum(normed_terms.astype(jnp.bfloat16), "dp").astype(jnp.float32)
+    down_terms = plain_dot(hidden_act, g_down).astype(jnp.bfloat16)
+    down_part = scatter_sum(down_terms, "dp").astype(jnp.float32)
+    feed_terms = jnp.concatenate(
+        [
+            outer_dot(gate_back, normed_group),
+            outer_dot(up_back, normed_group),
+            outer_dot(hidden_act, cot_group),
+        ],
+        1,
+    ).astype(jnp.bfloat16)
+    feed_grads = scatter_sum(feed_terms, "fsdp").astype(jnp.float32)
     layer_out = (middle + down_part).astype(jnp.bfloat16)
     grad_middle = cotangent.astype(jnp.float32) + norm_back(
         normed_part, middle, scale_ffn, gain_ffn
     )
     middle_bf = grad_middle.astype(jnp.bfloat16)
-    grad_attended = proj_dot(middle_bf, weights_back[0][QKV:]).astype(jnp.bfloat16)
+    grad_attended = proj_dot(middle_bf, w_out).astype(jnp.bfloat16)
     grad_attended = grad_attended.reshape(1, rows_here, KV_HEADS, repeat_count, HEAD_DIM)
     scores_again = attend_scores(query_bf, key_bf, allowed)
     soft = jnp.exp(scores_again - log_total)
@@ -165,47 +183,32 @@
         -1,
     )
     projected_bf = grad_projected.astype(jnp.bfloat16)
-    grad_inputs = plain_dot(projected_bf, weights_back[0][:QKV])
+    grad_inputs = plain_dot(projected_bf, w_qkv)
     grad_tokens = (grad_middle + norm_back(grad_inputs, resid_in, scale_att, gain_att)).astype(
         jnp.bfloat16
     )
     attention_term = jnp.concatenate(
         [outer_dot(projected_bf, normed_att), outer_dot(attended, middle_bf)], 0
     )
-    grad_attention = lax.psum_scatter(
-        attention_term, ("dp", "fsdp"), scatter_dimension=0, tiled=True
-    )
-    feed_grads = lax.psum_scatter(
-        jnp.stack(
-            [
-                outer_dot(gate_back, normed_ffn),
-                outer_dot(up_back, normed_ffn),
-                outer_dot(hidden_act, cotangent),
-            ],
-            1,
-        ),
-        ("dp", "fsdp"),
-        scatter_dimension=0,
-        tiled=True,
-    )
-    small_sums = lax.psum(
-        (
+    grad_attention = scatter_sum(attention_term.astype(jnp.bfloat16), BOTH).astype(jnp.float32)
+    small_terms = jnp.concatenate(
+        [
             jnp.sum(grad_inputs * resid_in * scale_att, 0),
             jnp.sum(normed_part * middle * scale_ffn, 0),
             jnp.sum(grad_projected, 0),
-        ),
-        ("dp", "fsdp"),
-    )
+        ]
+    )
+    small_sums = jnp.sum(gather(small_terms[None], BOTH), 0)
     return (
         layer_out,
         grad_tokens,
-        small_sums[0],
-        small_sums[1],
-        small_sums[2],
+        small_sums[:width],
+        small_sums[width : 2 * width],
+        small_sums[2 * width :],
         grad_attention,
-        feed_grads[:, 0],
-        feed_grads[:, 1],
-        feed_grads[:, 2],
+        feed_grads[:, :width],
+        feed_grads[:, width : 2 * width],
+        feed_grads[:, 2 * width :],
     )
 
 

time: 1100 us -> 543 us (0.49)
  waiting for transfers between devices: 909 us -> 428 us
  matrix products: 72.5 us -> 40.1 us
  other arithmetic: 43.5 us -> 14.1 us
    reduce_scatter x2 -> x3, waiting for transfers between devices: 628 us -> 249 us  [scatter_sum(): return lax.psum_scatter(terms, axes, scatter_dimension=0, tiled=True)]
    all_gather x4, waiting for transfers between devices: 279 us -> 177 us  [gather(): return lax.all_gather(shard, axes, axis=0, tiled=True)]
    psum x1 -> x0, blocking collectives: 49.4 us -> none  [on_device(): lax.psum((jnp.sum(grad_inputs * resid_in * scale_att, 0), jnp.sum(normed_...]
    all_gather x0 -> x1, blocking collectives: none -> 40.6 us  [gather(): return lax.all_gather(shard, axes, axis=0, tiled=True)]
    another operation x2 -> x1, other arithmetic: 34.8 us -> 0.23 us  [the longest x1 34.6 us: on_device(): jnp.stack([outer_dot(gate_back, normed_ffn), outer_dot(up_back, normed_ff...]
    dot_general x5, matrix products: 23.3 us -> 7.85 us  [outer_dot(): lax.dot_general(left, right, (((0,), (0,)), ((), ())), preferred_element_...]
  transfers between devices with their start and end apart: 6 -> 8, of which waited for: 6 -> 7; matrix products, arithmetic and copies ran while one was open for 5% -> 8% of each run, Pallas kernels for 0% -> 0%
where the time goes in v1:
time: 543 us; the launch traced here: 542 us
  waiting for transfers between devices  428 us (79%)
  blocking collectives  40.6 us (7%)
  matrix products  40.1 us (7%)
  between operations  14.6 us (3%)
  other arithmetic  14.1 us (3%)
    reduce_scatter x3, waiting for transfers between devices, scatter_sum(): return lax.psum_scatter(terms, axes, scatter_dimension=0, tiled=True)  249 us
    all_gather x4, waiting for transfers between devices, gather(): return lax.all_gather(shard, axes, axis=0, tiled=True)  177 us
    all_gather x1, blocking collectives, gather(): return lax.all_gather(shard, axes, axis=0, tiled=True)  40.6 us
    dot_general x5, matrix products, proj_dot(): lax.dot_general(left, right, (((1,), (1,)), ((), ())), preferred_element_...  16.4 us
    dot_general x5, matrix products, plain_dot(): return jnp.dot(left, right, preferred_element_type=jnp.float32)  14 us
  transfers between devices with their start and end apart: 8, of which 7 were waited for; matrix products, arithmetic and copies ran while one was open for 8% of the time, Pallas kernels for 0%

profile of v1, /device:TPU:0, one launch (start us, length us, event | category | flops | bytes accessed | tf_op | source)
XLA Modules:
  0.0 542.2 jit_solution(10048644469187946826)
XLA Ops:
  7.2 0.0 all-gather.7.cloned.1.call-start
  7.3 0.7 all-gather.7.cloned.1.call-update
  8.0 0.0 all-gather.13.cloned.1.call-start
  8.0 0.7 all-gather.13.cloned.1.call-update
  8.7 0.0 all-gather.11.cloned.1.call-start
  8.7 2.1 pad_maximum_fusion.2
  10.9 0.0 all-gather.9.cloned.1.call-start
  10.9 0.2 convert_reduce_fusion
  11.1 0.1 multiply_cosine_fusion
  11.3 0.1 fusion.40
  11.4 0.1 fusion.62
  11.5 62.5 %all-gather.7.cloned.1.call-done = bf16[2048,896]{1,0:T(8,128)(2,1)} async-done(((bf16[64,896]{1,0:T(8,128)(2,1)}), bf16[2048,896]{1,0:T(8,128)(2,1)}) %all-gather.7.cloned.1.call-update) | async-done | bytes 3670032 | tf_op jit(solution)/shard_map/all_gather | solution.py:78
  74.1 2.4 convolution_add_fusion
  76.5 0.1 copy.53
  76.6 0.2 copy.56
  76.8 0.1 copy.54
  77.0 0.1 fusion.51
  77.1 0.4 exponential_reduce_fusion
  77.5 0.3 convolution_convert_fusion.6
  77.8 2.0 multiply_reduce_fusion.1
  79.8 0.8 multiply_convert_fusion.2
  80.6 0.0 reduce-scatter.9.cloned.1.call-start
  80.7 40.6 %all-gather.13.cloned.1.call-done = bf16[1024,896]{1,0:T(8,128)(2,1)} async-done(((bf16[128,896]{1,0:T(8,128)(2,1)}), bf16[1024,896]{1,0:T(8,128)(2,1)}) %all-gather.13.cloned.1.call-update) | async-done | bytes 1835024 | tf_op jit(solution)/shard_map/all_gather | solution.py:78
  121.3 29.5 %all-gather.11.cloned.1.call-done = bf16[608,2688]{1,0:T(8,128)(2,1)} async-done(((bf16[152,2688]{1,0:T(8,128)(2,1)}), bf16[608,2688]{1,0:T(8,128)(2,1)}) %all-gather.11.cloned.1.call-update) | async-done | bytes 3268624 | tf_op jit(solution)/shard_map/all_gather | solution.py:78
  150.8 4.8 fusion.20
  155.6 44.2 %all-gather.9.cloned.1.call-done = bf16[1024,896]{1,0:T(8,128)(2,1)} async-done(((bf16[128,896]{1,0:T(8,128)(2,1)}), bf16[1024,896]{1,0:T(8,128)(2,1)}) %all-gather.9.cloned.1.call-update) | async-done | bytes 1835024 | tf_op jit(solution)/shard_map/all_gather | solution.py:78
  199.8 3.4 fusion.24
  203.3 0.7 copy-done.13
  203.9 3.7 fusion.4
  207.7 1.8 fusion.26
  209.5 3.1 add_convert_fusion
  212.6 0.0 reduce-scatter.7.cloned.1.call-start
  212.7 4.6 convolution_convert_fusion.1
  217.3 0.2 reduce-scatter.13.cloned.1.call-start
  217.6 3.6 convolution_convert_fusion.3
  221.2 1.5 convolution_convert_fusion.4
  222.7 1.5 convolution_convert_fusion.5
  224.2 1.9 pad_maximum_fusion.1
  226.1 0.0 reduce-scatter.11.cloned.1.call-start
  226.1 52.0 %reduce-scatter.9.cloned.1.call-done = bf16[128,896]{1,0:T(8,128)(2,1)} async-done(((bf16[1024,896]{1,0:T(8,128)(2,1)}), bf16[128,896]{1,0:T(8,128)(2,1)}) %reduce-scatter.9.cloned.1.call-update) | async-done | bytes 229392 | tf_op jit(solution)/shard_map/reduce_scatter | solution.py:82
  278.1 1.1 fusion.37
  279.3 68.0 %reduce-scatter.7.cloned.1.call-done = bf16[128,896]{1,0:T(8,128)(2,1)} async-done(((bf16[1024,896]{1,0:T(8,128)(2,1)}), bf16[128,896]{1,0:T(8,128)(2,1)}) %reduce-scatter.7.cloned.1.call-update) | async-done | bytes 229392 | tf_op jit(solution)/shard_map/reduce_scatter | solution.py:82
  347.3 1.9 fusion.34
  349.2 2.0 fusion.17
  351.2 0.2 copy.59
  351.4 0.3 multiply_reduce_fusion
  351.7 0.2 fusion.39
  352.0 0.2 fusion.73
  352.3 0.1 fusion.52
  352.4 0.3 broadcast_multiply_fusion
  352.7 0.3 fusion.55
  353.0 0.6 convolution_convert_fusion.2
  353.6 0.8 convolution_convert_fusion
  354.4 2.1 pad_maximum_fusion
  356.5 0.2 fusion.53
  356.8 2.5 fusion.49
  359.3 40.6 %all-gather.1 = f32[32,1,2944]{2,1,0:T(1,128)S(1)} all-gather(f32[1,1,2944]{2,1,0:T(1,128)S(1)} %reshape.461), channel_id=2, replica_groups=mesh['dp'=8,'fsdp'=4] {'dp','fsdp'}, dimensions={0}, use_global_device_ids=true | all-gather | bytes 388608 | tf_op jit(solution)/shard_map/all_gather | solution.py:78
  399.9 0.2 reduce_sum.109
  400.1 0.6 slice.107
  400.7 0.6 fusion.72
  401.3 0.9 fusion.46
  402.2 2.3 fusion.69
  404.5 129.2 %reduce-scatter.11.cloned.1.call-done = bf16[64,896]{1,0:T(8,128)(2,1)} async-done(((bf16[2048,896]{1,0:T(8,128)(2,1)}), bf16[64,896]{1,0:T(8,128)(2,1)}) %reduce-scatter.11.cloned.1.call-update) | async-done | bytes 114704 | tf_op jit(solution)/shard_map/reduce_scatter | solution.py:82
  533.8 1.6 convert_element_type.145
  (56 shorter events, 0.5 us)
Async XLA Ops:
  7.2 3.7 copy-start.4
  7.2 4.1 copy-start
  7.2 66.9 %copy-start.3 = (f32[896]{0:T(1024)S(1)}, f32[896]{0:T(1024)}, u32[]{:S(2)}) copy-start(f32[896]{0:T(1024)} %param.13) | copy-start | bytes 10756
  7.2 66.8 %copy-start.8 = (f32[1152]{0:T(1024)S(1)}, f32[1152]{0:T(1024)}, u32[]{:S(2)}) copy-start(f32[1152]{0:T(1024)} %param.15) | copy-start | bytes 13828
  7.2 66.8 %all-gather.7.cloned.1.call-start = ((), (), s32[]{:S(2)}) async-start(), calls=%async_computation.4 | async-start | bytes 3784704 | tf_op jit(solution)/shard_map/all_gather | solution.py:78
  8.0 113.3 %all-gather.13.cloned.1.call-start = ((), (), s32[]{:S(2)}) async-start(), calls=%async_computation.8 | async-start | bytes 2064384 | tf_op jit(solution)/shard_map/all_gather | solution.py:78
  8.7 142.1 %all-gather.11.cloned.1.call-start = ((), (), s32[]{:S(2)}) async-start(), calls=%async_computation.6 | async-start | bytes 4085760 | tf_op jit(solution)/shard_map/all_gather | solution.py:78
  10.9 189.0 %all-gather.9.cloned.1.call-start = ((), (), s32[]{:S(2)}) async-start(), calls=%async_computation.5 | async-start | bytes 2064384 | tf_op jit(solution)/shard_map/all_gather | solution.py:78
  77.5 2.3 copy-start.2
  80.6 197.5 %reduce-scatter.9.cloned.1.call-start = ((), (), s32[]{:S(2)}) async-start(), calls=%async_computation.9 | async-start | bytes 2064384 | tf_op jit(solution)/shard_map/reduce_scatter | solution.py:82
  199.8 3.4 copy-start.5
  199.8 3.4 copy-start.6
  199.8 4.1 copy-start.13
  207.7 1.8 copy-start.11
  207.7 1.8 copy-start.9
  212.6 134.6 %reduce-scatter.7.cloned.1.call-start = ((), (), s32[]{:S(2)}) async-start(), calls=%async_computation.7 | async-start | bytes 2064384 | tf_op jit(solution)/shard_map/reduce_scatter | solution.py:82
  217.3 184.9 %reduce-scatter.13.cloned.1.call-start = ((), (), s32[]{:S(2)}) async-start(), calls=%async_computation.11 | async-start | bytes 4085760
  217.5 3.7 copy-start.7
  217.6 3.7 copy-start.10
  221.2 1.5 copy-start.12
  226.1 121.2 %copy-start.1 = (bf16[128,896]{1,0:T(8,128)(2,1)S(1)}, bf16[128,896]{1,0:T(8,128)(2,1)}, u32[]{:S(2)}) copy-start(bf16[128,896]{1,0:T(8,128)(2,1)} %param.11) | copy-start | bytes 688132
  226.1 307.7 %reduce-scatter.11.cloned.1.call-start = ((), (), s32[]{:S(2)}) async-start(), calls=%async_computation.10 | async-start | bytes 3784704 | tf_op jit(solution)/shard_map/reduce_scatter | solution.py:82
Sparse Core Ops, SparseCore 0:
  10.9 63.1 all-gather.6
  76.2 44.9 all-gather.12
  122.8 27.9 all-gather.10
  153.4 46.3 all-gather.8
  212.7 65.3 reduce-scatter.8
  281.5 65.7 reduce-scatter.6
  349.8 40.0 reduce-scatter.12
  392.2 141.5 reduce-scatter.10

commit v2 on v1

--- a/solution.py
+++ b/solution.py
@@ -1,7 +1,10 @@
 import jax
 import jax.numpy as jnp
+import functools
 from jax import lax
-from jax.sharding import PartitionSpec as P
+from jax.experimental import pallas as pl
+from jax.experimental.pallas import tpu as pltpu
+from jax.sharding import Mesh, PartitionSpec as P
 
 HEADS = 14
 KV_HEADS = 2
@@ -71,7 +74,10 @@
     )
 
 
-BOTH = ("dp", "fsdp")
+PLANE = ("y", "x", "c")
+BOTH = ("z",) + PLANE
+OTHERS = ((1, 1), (0, 1), (1, 0))
+MESH_ID = pl.DeviceIdType.MESH
 
 
 def gather(shard, axes):
@@ -82,15 +88,243 @@
     return lax.psum_scatter(terms, axes, scatter_dimension=0, tiled=True)
 
 
+def here():
+    return tuple(lax.axis_index(name) for name in BOTH)
+
+
+def at_device(z, y, x, c):
+    return {"z": z, "y": y, "x": x, "c": c}
+
+
+def greet(count):
+    z, y, x, c = here()
+    barrier = pltpu.get_barrier_semaphore()
+    targets = [at_device(lax.rem(z + k, count), y, x, c) for k in range(1, count)]
+    targets += [at_device(z, y ^ dy, x ^ dx, c) for dy, dx in OTHERS]
+    targets.append(at_device(z, y, x, 1 - c))
+    for target in targets:
+        pl.semaphore_signal(barrier, inc=1, device_id=target, device_id_type=MESH_ID)
+    pl.semaphore_wait(barrier, len(targets))
+
+
+def remote(source, target, send, recv, device):
+    return pltpu.make_async_remote_copy(
+        src_ref=source,
+        dst_ref=target,
+        send_sem=send,
+        recv_sem=recv,
+        device_id=device,
+        device_id_type=MESH_ID,
+    )
+
+
+def gather_kernel(count, shard, out, own_sem, z_send, z_recv, p_send, p_recv, c_send, c_recv):
+    z, y, x, c = here()
+    greet(count)
+    slot = z if count > 1 else 0
+    own = pltpu.make_async_copy(shard, out.at[slot, y, x, c], own_sem)
+    own.start()
+    along_z = []
+    for k in range(1, count):
+        copy = remote(
+            shard,
+            out.at[slot, y, x, c],
+            z_send.at[k - 1],
+            z_recv.at[k - 1],
+            at_device(lax.rem(z + k, count), y, x, c),
+        )
+        copy.start()
+        along_z.append(copy)
+    sent = []
+    for k in range(count):
+        if k:
+            along_z[k - 1].wait_recv()
+        held = lax.rem(z - k + count, count) if count > 1 else 0
+        block = out.at[held, y, x, c]
+        source = block if k else shard
+        for j, (dy, dx) in enumerate(OTHERS):
+            copy = remote(
+                source, block, p_send.at[k, j], p_recv.at[k, j], at_device(z, y ^ dy, x ^ dx, c)
+            )
+            copy.start()
+            sent.append((copy, k, j, held))
+        copy = remote(source, block, c_send.at[k, 3], c_recv.at[k, 3], at_device(z, y, x, 1 - c))
+        copy.start()
+        along_z.append(copy)
+    passed = []
+    for copy, k, j, held in sent:
+        dy, dx = OTHERS[j]
+        copy.wait_recv()
+        block = out.at[held, y ^ dy, x ^ dx, c]
+        onward = remote(block, block, c_send.at[k, j], c_recv.at[k, j], at_device(z, y, x, 1 - c))
+        onward.start()
+        passed.append(onward)
+    for copy, k, j, held in sent:
+        copy.wait_send()
+    for at, copy in enumerate(along_z):
+        copy.wait_send()
+        if at >= count - 1:
+            copy.wait_recv()
+    for copy in passed:
+        copy.wait()
+    own.wait()
+
+
+def kernel_gather(shard, count, ident):
+    rows, width = shard.shape
+    dma = pltpu.SemaphoreType.DMA
+    out = pl.pallas_call(
+        functools.partial(gather_kernel, count),
+        out_shape=jax.ShapeDtypeStruct((count, 2, 2, 2, rows, width), shard.dtype),
+        in_specs=[pl.BlockSpec(memory_space=pltpu.VMEM)],
+        out_specs=pl.BlockSpec(memory_space=pl.ANY),
+        scratch_shapes=[
+            dma(()),
+            dma((3,)),
+            dma((3,)),
+            dma((count, 3)),
+            dma((count, 3)),
+            dma((count, 4)),
+            dma((count, 4)),
+        ],
+        compiler_params=pltpu.CompilerParams(collective_id=ident, has_side_effects=True),
+        cost_estimate=pl.CostEstimate(
+            flops=20_000_000_000, bytes_accessed=8 * count * rows * width * 2, transcendentals=0
+        ),
+    )(shard)
+    return out.reshape(count * 8 * rows, width)
+
+
+def scatter_kernel(
+    count, terms, out, c_buf, s_buf, p_buf, total, zs_buf, zr_buf,
+    c_send, c_recv, p_send, p_recv, z_send, z_recv,
+):
+    z, y, x, c = here()
+    greet(count)
+    pieces = OTHERS + ((0, 0),)
+    across = []
+    for j, (dy, dx) in enumerate(pieces):
+        copy = remote(
+            terms.at[:, y ^ dy, x ^ dx, 1 - c],
+            c_buf.at[j],
+            c_send.at[j],
+            c_recv.at[j],
+            at_device(z, y, x, 1 - c),
+        )
+        copy.start()
+        across.append(copy)
+    plane = []
+    for j, (dy, dx) in enumerate(pieces):
+        across[j].wait_recv()
+        for k in range(count):
+            pair = terms[k, y ^ dy, x ^ dx, c].astype(jnp.float32) + c_buf[j, k].astype(jnp.float32)
+            if j < 3:
+                s_buf[j, k] = pair.astype(jnp.bfloat16)
+            else:
+                total[k] = pair
+        if j < 3:
+            copy = remote(
+                s_buf.at[j],
+                p_buf.at[j],
+                p_send.at[j],
+                p_recv.at[j],
+                at_device(z, y ^ dy, x ^ dx, c),
+            )
+            copy.start()
+            plane.append(copy)
+    for copy in plane:
+        copy.wait_recv()
+    if count == 1:
+        out[...] = (
+            total[0]
+            + p_buf[0, 0].astype(jnp.float32)
+            + p_buf[1, 0].astype(jnp.float32)
+            + p_buf[2, 0].astype(jnp.float32)
+        )
+    along = []
+    for k in range(1, count):
+        other = lax.rem(z + k, count)
+        zs_buf[k - 1] = (
+            total[other]
+            + p_buf[0, other].astype(jnp.float32)
+            + p_buf[1, other].astype(jnp.float32)
+            + p_buf[2, other].astype(jnp.float32)
+        ).astype(jnp.bfloat16)
+        copy = remote(
+            zs_buf.at[k - 1],
+            zr_buf.at[k - 1],
+            z_send.at[k - 1],
+            z_recv.at[k - 1],
+            at_device(other, y, x, c),
+        )
+        copy.start()
+        along.append(copy)
+    if count > 1:
+        kept = (
+            total[z]
+            + p_buf[0, z].astype(jnp.float32)
+            + p_buf[1, z].astype(jnp.float32)
+            + p_buf[2, z].astype(jnp.float32)
+        )
+        for k in range(1, count):
+            along[k - 1].wait_recv()
+            kept = kept + zr_buf[k - 1].astype(jnp.float32)
+        out[...] = kept
+    for copy in across + plane + along:
+        copy.wait_send()
+
+
+def kernel_scatter(terms, count, ident):
+    rows, width = terms.shape[0] // (8 * count), terms.shape[1]
+    dma = pltpu.SemaphoreType.DMA
+    block = (rows, width)
+    extra = block if count > 1 else (16, 128)
+    return pl.pallas_call(
+        functools.partial(scatter_kernel, count),
+        out_shape=jax.ShapeDtypeStruct(block, jnp.float32),
+        in_specs=[pl.BlockSpec(memory_space=pltpu.VMEM)],
+        out_specs=pl.BlockSpec(memory_space=pltpu.VMEM),
+        scratch_shapes=[
+            pltpu.VMEM((4, count) + block, jnp.bfloat16),
+            pltpu.VMEM((3, count) + block, jnp.bfloat16),
+            pltpu.VMEM((3, count) + block, jnp.bfloat16),
+            pltpu.VMEM((count,) + block, jnp.float32),
+            pltpu.VMEM((3,) + extra, jnp.bfloat16),
+            pltpu.VMEM((3,) + extra, jnp.bfloat16),
+            dma((4,)),
+            dma((4,)),
+            dma((3,)),
+            dma((3,)),
+            dma((3,)),
+            dma((3,)),
+        ],
+        compiler_params=pltpu.CompilerParams(collective_id=ident, has_side_effects=True),
+        cost_estimate=pl.CostEstimate(
+            flops=20_000_000_000, bytes_accessed=8 * count * rows * width * 2, transcendentals=0
+        ),
+    )(terms.reshape((count, 2, 2, 2) + block))
+
+
+def gather_over(shard, axes, ident, kernels):
+    if not kernels:
+        return gather(shard, axes)
+    return kernel_gather(shard, lax.axis_size("z") if axes == BOTH else 1, ident)
+
+
+def scatter_over(terms, axes, ident, kernels):
+    if not kernels:
+        return scatter_sum(terms, axes).astype(jnp.float32)
+    return kernel_scatter(terms, lax.axis_size("z") if axes == BOTH else 1, ident)
+
+
 def on_device(
-    tokens, cotangent, segments, gain_att, gain_ffn, qkv_bias, w_attention, w_gate, w_up, w_down
+    kernels, tokens, cotangent, segments, gain_att, gain_ffn, qkv_bias, w_attention, w_gate, w_up, w_down
 ):
-    w_all = gather(w_attention, BOTH)
+    w_all = gather_over(w_attention, BOTH, 0, kernels)
     w_qkv, w_out = w_all[:QKV], w_all[QKV:]
     width = tokens.shape[1]
-    w_feed = gather(jnp.concatenate([w_gate, w_up, w_down], 1), "fsdp")
+    w_feed = gather(jnp.concatenate([w_gate, w_up, w_down], 1), "z")
     g_gate, g_up, g_down = w_feed[:, :width], w_feed[:, width : 2 * width], w_feed[:, 2 * width :]
-    cot_group = gather(cotangent, "dp")
     rows_here = tokens.shape[0]
     q_width = HEADS * HEAD_DIM
     kv_width = KV_HEADS * HEAD_DIM
@@ -121,7 +355,8 @@
     middle = resid_in + plain_dot(attended, w_out)
     scale_ffn = lax.rsqrt(jnp.mean(middle * middle, -1, keepdims=True) + EPS)
     normed_ffn = (middle * scale_ffn * gain_ffn).astype(jnp.bfloat16)
-    normed_group = gather(normed_ffn, "dp")
+    pair_group = gather_over(jnp.concatenate([normed_ffn, cotangent], 1), PLANE, 1, kernels)
+    normed_group, cot_group = pair_group[:, :width], pair_group[:, width:]
     gate_pre = proj_dot(normed_group, g_gate)
     up_pre = proj_dot(normed_group, g_up)
     grad_hidden = proj_dot(cot_group, g_down)
@@ -132,9 +367,9 @@
     ).astype(jnp.bfloat16)
     up_back = (grad_hidden * gate_pre * sigmoid_gate).astype(jnp.bfloat16)
     normed_terms = plain_dot(gate_back, g_gate) + plain_dot(up_back, g_up)
-    normed_part = scatter_sum(normed_terms.astype(jnp.bfloat16), "dp").astype(jnp.float32)
-    down_terms = plain_dot(hidden_act, g_down).astype(jnp.bfloat16)
-    down_part = scatter_sum(down_terms, "dp").astype(jnp.float32)
+    pair_terms = jnp.concatenate([normed_terms, plain_dot(hidden_act, g_down)], 1)
+    pair_sums = scatter_over(pair_terms.astype(jnp.bfloat16), PLANE, 2, kernels)
+    normed_part, down_part = pair_sums[:, :width], pair_sums[:, width:]
     feed_terms = jnp.concatenate(
         [
             outer_dot(gate_back, normed_group),
@@ -143,7 +378,7 @@
         ],
         1,
     ).astype(jnp.bfloat16)
-    feed_grads = scatter_sum(feed_terms, "fsdp").astype(jnp.float32)
+    feed_grads = scatter_sum(feed_terms, "z").astype(jnp.float32)
     layer_out = (middle + down_part).astype(jnp.bfloat16)
     grad_middle = cotangent.astype(jnp.float32) + norm_back(
         normed_part, middle, scale_ffn, gain_ffn
@@ -190,7 +425,7 @@
     attention_term = jnp.concatenate(
         [outer_dot(projected_bf, normed_att), outer_dot(attended, middle_bf)], 0
     )
-    grad_attention = scatter_sum(attention_term.astype(jnp.bfloat16), BOTH).astype(jnp.float32)
+    grad_attention = scatter_over(attention_term.astype(jnp.bfloat16), BOTH, 3, kernels)
     small_terms = jnp.concatenate(
         [
             jnp.sum(grad_inputs * resid_in * scale_att, 0),
@@ -198,13 +433,16 @@
             jnp.sum(grad_projected, 0),
         ]
     )
-    small_sums = jnp.sum(gather(small_terms[None], BOTH), 0)
+    small_block = jnp.pad(small_terms, (0, -small_terms.size % 1024)).reshape(-1, 128)
+    small_sums = jnp.sum(
+        gather_over(small_block, BOTH, 4, kernels).reshape(-1, small_block.size), 0
+    )
     return (
         layer_out,
         grad_tokens,
         small_sums[:width],
         small_sums[width : 2 * width],
-        small_sums[2 * width :],
+        small_sums[2 * width : small_terms.size],
         grad_attention,
         feed_grads[:, :width],
         feed_grads[:, width : 2 * width],
@@ -213,32 +451,35 @@
 
 
 def solution(mesh):
+    dp, fsdp = mesh.shape["dp"], mesh.shape["fsdp"]
+    kernels = (dp, fsdp) == (8, 4)
+    finer = Mesh(mesh.devices.reshape(dp // 2, 2, fsdp // 2, 2), BOTH)
     placed = (
-        P(("dp", "fsdp"), None),
-        P(("dp", "fsdp"), None),
-        P(("dp", "fsdp"), None),
+        P(BOTH, None),
+        P(BOTH, None),
+        P(BOTH, None),
         P(),
         P(),
         P(),
-        P(("dp", "fsdp"), None),
-        P(("dp", "fsdp"), None),
-        P(("dp", "fsdp"), None),
-        P(("dp", "fsdp"), None),
+        P(BOTH, None),
+        P(BOTH, None),
+        P(BOTH, None),
+        P(BOTH, None),
     )
     return jax.shard_map(
-        on_device,
-        mesh=mesh,
+        functools.partial(on_device, kernels),
+        mesh=finer,
         in_specs=placed,
         out_specs=(
-            P(("dp", "fsdp"), None),
-            P(("dp", "fsdp"), None),
+            P(BOTH, None),
+            P(BOTH, None),
             P(),
             P(),
             P(),
-            P(("dp", "fsdp"), None),
-            P(("dp", "fsdp"), None),
-            P(("dp", "fsdp"), None),
-            P(("dp", "fsdp"), None),
+            P(BOTH, None),
+            P(BOTH, None),
+            P(BOTH, None),
+            P(BOTH, None),
         ),
         check_vma=False,
     )

time: 543 us -> 231 us (0.43)
  waiting for transfers between devices: 428 us -> 6.49 us
  Pallas kernels: 0 us -> 153 us
  blocking collectives: 40.6 us -> 0 us
  matrix products: 40.1 us -> 32.5 us
    reduce_scatter x3 -> x0, waiting for transfers between devices: 249 us -> none  [scatter_sum(): return lax.psum_scatter(terms, axes, scatter_dimension=0, tiled=True)]
    all_gather x4 -> x1, waiting for transfers between devices: 177 us -> 6.46 us  [gather(): return lax.all_gather(shard, axes, axis=0, tiled=True)]
    pallas_call x0 -> x5, Pallas kernels: none -> 153 us  [the longest x3 79.1 us: kernel_gather(): pl.pallas_call(functools.partial(gather_kernel, count), out_shape=jax.Sha...]
    all_gather x1 -> x0, blocking collectives: 40.6 us -> none  [gather(): return lax.all_gather(shard, axes, axis=0, tiled=True)]
  transfers between devices with their start and end apart: 8 -> 2, of which waited for: 7 -> 1; matrix products, arithmetic and copies ran while one was open for 8% -> 8% of each run, Pallas kernels for 0% -> 54%
where the time goes in v2:
time: 231 us
  Pallas kernels  153 us (66%)
  matrix products  32.5 us (14%)
  other arithmetic  17.6 us (8%)
  between operations  14.5 us (6%)
  waiting for transfers between devices  6.49 us (3%)
  local copies, waits for them, and re-layouts  6.48 us (3%)
    pallas_call x3, Pallas kernels, kernel_gather(): pl.pallas_call(functools.partial(gather_kernel, count), out_shape=jax.Sha...  79.1 us
    pallas_call x2, Pallas kernels, kernel_scatter(): pl.pallas_call(functools.partial(scatter_kernel, count), out_shape=jax.Sh...  74.1 us
    dot_general x5, matrix products, proj_dot(): lax.dot_general(left, right, (((1,), (1,)), ((), ())), preferred_element_...  12.1 us
    dot_general x5, matrix products, plain_dot(): return jnp.dot(left, right, preferred_element_type=jnp.float32)  9.75 us
    dot_general x5, matrix products, outer_dot(): lax.dot_general(left, right, (((0,), (0,)), ((), ())), preferred_element_...  8.77 us
    all_gather x1, waiting for transfers between devices, gather(): return lax.all_gather(shard, axes, axis=0, tiled=True)  6.46 us
  transfers between devices with their start and end apart: 2, of which 1 were waited for; matrix products, arithmetic and copies ran while one was open for 8% of the time, Pallas kernels for 54%

profile of v2, /device:TPU:0, one launch (start us, length us, event | category | flops | bytes accessed | tf_op | source)
XLA Modules:
  0.0 230.8 jit_solution(8916653035078851480)
XLA Ops:
  7.2 0.0 all-gather.2.cloned.1.call-start
  7.2 2.1 pad_maximum_fusion.3
  9.4 0.0 all-gather.2.cloned.1.call-update
  9.4 0.0 reduce-scatter.4.cloned.1.call-start
  9.4 0.9 convert_reduce_fusion
  10.4 0.1 fusion.38
  10.5 0.5 multiply_multiply_fusion
  11.0 30.0 %shard_map.169 = bf16[4,2,2,2,64,896]{5,4,3,2,1,0:T(8,128)(2,1)} custom-call(bf16[64,896]{1,0:T(8,128)(2,1)} %shard.1), custom_call_target="tpu_custom_call" | custom-call | flops 20000000000 | bytes 3670016 | tf_op jit(solution)/shard_map/pallas_call | solution.py:176
  41.1 0.0 copy-start.8
  41.1 2.4 %convolution_add_fusion = f32[128,1152]{1,0:T(8,128)S(1)} fusion(bf16[2048,896]{1,0:T(8,128)(2,1)} %bitcast.110, f32[1152]{0:T(1024)S(1)} %copy-done.11, bf16[128,896]{1,0:T(8,128)(2,1)S(1)} %copy-done, f32[896]{0:T(1024)S(1)} %copy-done.7, f32[128]{0:T(128)S(1)} %get-tuple-element.34), kind=kOutput, calls=%fused_computation.5 | convolution fusion | flops 264847360 | bytes 2892288 | tf_op jit(solution)/shard_map/dot_general | solution.py:66
  43.5 0.1 copy.53
  43.6 0.2 copy.56
  43.9 0.1 copy.54
  44.0 0.1 multiply_cosine_fusion
  44.1 0.1 fusion.60
  44.3 0.1 fusion.49
  44.4 0.4 exponential_reduce_fusion
  44.8 0.3 convolution_convert_fusion.5
  45.1 2.0 multiply_reduce_fusion.3
  47.1 0.1 multiply_convert_fusion.4
  47.2 0.8 pad_maximum_fusion.5.shard
  48.0 27.4 %shard_map.170 = bf16[1,2,2,2,128,1792]{5,4,3,2,1,0:T(8,128)(2,1)} custom-call(bf16[128,1792]{1,0:T(8,128)(2,1)} %pad_maximum_fusion.5.shard), custom_call_target="tpu_custom_call" | custom-call | flops 20000000000 | bytes 3670016 | tf_op jit(solution)/shard_map/pallas_call | solution.py:176
  75.5 6.5 %all-gather.2.cloned.1.call-done = bf16[608,2688]{1,0:T(8,128)(2,1)} async-done(((bf16[152,2688]{1,0:T(8,128)(2,1)}), bf16[608,2688]{1,0:T(8,128)(2,1)}) %all-gather.2.cloned.1.call-update) | async-done | bytes 3268624 | tf_op jit(solution)/shard_map/all_gather | solution.py:84
  81.9 3.4 %fusion.24 = f32[1024,608]{0,1:T(8,128)S(1)} fusion(bf16[1024,1792]{1,0:T(8,128)(2,1)} %bitcast.134, bf16[608,2688]{1,0:T(8,128)(2,1)} %all-gather.2.cloned.1.call-done), kind=kOutput, calls=%fused_computation.35 | convolution fusion | flops 1115684864 | bytes 5414912 | tf_op jit(solution)/shard_map/dot_general | solution.py:66
  85.4 0.5 copy-done.12
  85.8 1.5 fusion.26
  87.3 2.8 %multiply_convert_fusion.1 = (bf16[1024,608]{0,1:T(8,128)(2,1)S(1)}, bf16[1024,608]{0,1:T(8,128)(2,1)S(1)}, bf16[1024,608]{0,1:T(8,128)(2,1)S(1)}) fusion(f32[1024,608]{0,1:T(8,128)S(1)} %fusion.24, f32[1024,608]{0,1:T(8,128)S(1)} %fusion.26, bf16[608,2688]{1,0:T(8,128)(2,1)S(1)} %copy-done.10, bf16[1024,1792]{1,0:T(8,128)(2,1)S(1)} %bitcast.136), kind=kOutput, calls=%fused_computation.7 | convolution fusion | flops 1125646336 | bytes 11640832 | tf_op jit(solution)/shard_map/dot_general | solution.py:66
  90.2 2.5 %convolution_convert_fusion.3 = bf16[608,896]{1,0:T(8,128)(2,1)} fusion(bf16[1024,608]{0,1:T(8,128)(2,1)S(1)} %get-tuple-element.13, bf16[1024,1792]{1,0:T(8,128)(2,1)S(1)} %bitcast.137), kind=kOutput, calls=%fused_computation.20 | convolution fusion | flops 1116229632 | bytes 4169728 | tf_op jit(solution)/shard_map/dot_general | solution.py:72
  92.7 2.4 %convolution_convert_fusion.4 = bf16[608,896]{1,0:T(8,128)(2,1)} fusion(bf16[1024,608]{0,1:T(8,128)(2,1)S(1)} %get-tuple-element.14, bf16[1024,1792]{1,0:T(8,128)(2,1)S(1)} %bitcast.138), kind=kOutput, calls=%fused_computation.21 | convolution fusion | flops 1116229632 | bytes 4169728 | tf_op jit(solution)/shard_map/dot_general | solution.py:72
  95.1 2.5 %fusion.7 = bf16[608,896]{1,0:T(8,128)(2,1)} fusion(bf16[1024,608]{0,1:T(8,128)(2,1)S(1)} %get-tuple-element.15, bf16[1024,1792]{1,0:T(8,128)(2,1)S(1)} %bitcast.139), kind=kOutput, calls=%fused_computation.19 | convolution fusion | flops 1116229632 | bytes 4169728 | tf_op jit(solution)/shard_map/dot_general | solution.py:72
  97.6 1.8 convolution_convert_fusion.1
  99.4 1.8 fusion.28
  101.2 1.9 add_convert_fusion
  103.1 2.1 pad_maximum_fusion.terms
  105.3 28.6 %shard_map.171 = f32[128,1792]{1,0:T(8,128)} custom-call(bf16[1,2,2,2,128,1792]{5,4,3,2,1,0:T(8,128)(2,1)} %pad_maximum_fusion.terms), custom_call_target="tpu_custom_call" | custom-call | flops 20000000000 | bytes 3670016 | tf_op jit(solution)/shard_map/pallas_call | solution.py:282
  133.9 1.2 multiply_reduce_fusion.1
  135.1 2.0 subtract_add_fusion
  137.1 2.0 fusion.19
  139.1 0.2 copy.59
  139.3 0.3 multiply_reduce_fusion
  139.7 0.2 fusion.37
  139.9 0.3 broadcast_multiply_fusion
  140.2 0.2 fusion.71
  140.4 0.5 copy-done.1
  140.9 0.3 copy-done.2
  141.2 0.3 copy-done.3
  141.5 1.9 pad_maximum_fusion.2
  143.4 0.0 reduce-scatter.4.cloned.1.call-update
  143.6 0.1 fusion.50
  143.7 0.3 fusion.53
  144.0 0.6 convolution_convert_fusion.2
  144.6 0.8 convolution_convert_fusion
  145.3 2.1 pad_maximum_fusion.1
  147.5 45.5 %shard_map.173 = f32[64,896]{1,0:T(8,128)} custom-call(bf16[4,2,2,2,64,896]{5,4,3,2,1,0:T(8,128)(2,1)} %bitcast.109), custom_call_target="tpu_custom_call" | custom-call | flops 20000000000 | bytes 3670016 | tf_op jit(solution)/shard_map/pallas_call | solution.py:282
  193.0 0.2 fusion.51
  193.2 2.3 fusion.47
  195.5 0.6 fusion.65.shard
  196.1 21.6 %shard_map.172 = f32[4,2,2,2,24,128]{5,4,3,2,1,0:T(8,128)} custom-call(f32[24,128]{1,0:T(8,128)} %fusion.65.shard), custom_call_target="tpu_custom_call" | custom-call | flops 20000000000 | bytes 196608 | tf_op jit(solution)/shard_map/pallas_call | solution.py:176
  217.7 1.1 reduce_sum.109
  218.8 0.6 slice_bitcast_fusion.2
  219.4 0.6 slice_bitcast_fusion.1
  220.0 0.9 fusion.44
  220.9 2.3 %fusion.68 = (f32[152,896]{1,0:T(8,128)}, f32[152,896]{1,0:T(8,128)}, f32[152,896]{1,0:T(8,128)}) fusion(bf16[152,2688]{1,0:T(8,128)(2,1)} %reduce-scatter.4.cloned.1.call-done), kind=kLoop, calls=%fused_computation.125 | loop fusion | bytes 3268608 | tf_op jit(solution)/shard_map/slice | solution.py:449
  223.2 0.7 copy.72
  (40 shorter events, 0.3 us)
Async XLA Ops:
  7.2 3.2 %copy-start = (bf16[128,896]{1,0:T(8,128)(2,1)S(1)}, bf16[128,896]{1,0:T(8,128)(2,1)}, u32[]{:S(2)}) copy-start(bf16[128,896]{1,0:T(8,128)(2,1)} %param.10) | copy-start | bytes 688132
  7.2 74.7 %all-gather.2.cloned.1.call-start = ((), (), s32[]{:S(2)}) async-start(), calls=%async_computation.1 | async-start | bytes 4085760 | tf_op jit(solution)/shard_map/all_gather | solution.py:84
  9.4 211.5 %reduce-scatter.4.cloned.1.call-start = ((), (), s32[]{:S(2)}) async-start(), calls=%async_computation.2 | async-start | bytes 4085760
  11.0 30.0 %copy-start.7 = (f32[896]{0:T(1024)S(1)}, f32[896]{0:T(1024)}, u32[]{:S(2)}) copy-start(f32[896]{0:T(1024)} %param.13) | copy-start | bytes 10756
  11.0 30.0 %copy-start.11 = (f32[1152]{0:T(1024)S(1)}, f32[1152]{0:T(1024)}, u32[]{:S(2)}) copy-start(f32[1152]{0:T(1024)} %param.15) | copy-start | bytes 13828
  41.1 3.1 %copy-start.8 = (s32[1,128]{1,0:T(1,128)S(1)}, s32[1,128]{1,0:T(1,128)}, u32[]{:S(2)}) copy-start(s32[1,128]{1,0:T(1,128)} %param.12) | copy-start | bytes 1540
  44.4 2.7 %copy-start.6 = (f32[896]{0:T(1024)S(1)}, f32[896]{0:T(1024)}, u32[]{:S(2)}) copy-start(f32[896]{0:T(1024)} %param.14) | copy-start | bytes 10756
  44.8 2.4 %copy-start.4 = (bf16[128,896]{1,0:T(8,128)(2,1)S(1)}, bf16[128,896]{1,0:T(8,128)(2,1)}, u32[]{:S(2)}) copy-start(bf16[128,896]{1,0:T(8,128)(2,1)} %param.11) | copy-start | bytes 688132
  81.9 3.4 %copy-start.10 = (bf16[608,2688]{1,0:T(8,128)(2,1)S(1)}, bf16[608,2688]{1,0:T(8,128)(2,1)}, u32[]{:S(2)}) copy-start(bf16[608,2688]{1,0:T(8,128)(2,1)} %all-gather.2.cloned.1.call-done) | copy-start | bytes 9805828
  81.9 3.9 %copy-start.12 = (bf16[1,2,2,2,128,1792]{5,4,3,2,1,0:T(8,128)(2,1)S(1)}, bf16[1,2,2,2,128,1792]{5,4,3,2,1,0:T(8,128)(2,1)}, u32[]{:S(2)}) copy-start(bf16[1,2,2,2,128,1792]{5,4,3,2,1,0:T(8,128)(2,1)} %shard_map.170) | copy-start | bytes 11010052
  139.6 1.2 copy-start.1
  139.7 1.6 copy-start.2
  139.7 1.9 copy-start.3
  196.1 24.0 %copy-start.9 = (f32[128]{0:T(128)S(1)}, f32[128]{0:T(128)}, u32[]{:S(2)}) copy-start(f32[128]{0:T(128)} %get-tuple-element.33) | copy-start | bytes 1540
  217.7 5.5 %copy-start.5 = (f32[64,896]{1,0:T(8,128)S(1)}, f32[64,896]{1,0:T(8,128)}, u32[]{:S(2)}) copy-start(f32[64,896]{1,0:T(8,128)} %shard_map.173) | copy-start | bytes 688132
Sparse Core Ops, SparseCore 0:
  9.6 72.3 all-gather.1
  143.6 69.3 reduce-scatter.3
